TPU v7x, 32 devices: a whole 2x2x4 slice. The times are simulated.
32 devices in a mesh: seq: 8 (over y, x, core), fsdp: 4 (over z).
Axes of the slice: x: 2, y: 2, z: 4, core: 2. Of those that a mesh axis runs over, the one named last changes fastest.
Arguments:
- hidden: bfloat16 [8192, 3584], P(('seq', 'fsdp')), may hold values from -6 to 6
- queries: bfloat16 [8192, 2048], P(('seq', 'fsdp')), may hold values from -360 to 360
- kv_weights: bfloat16 [2, 3584, 1024], P(None, 'fsdp'), may hold values from -0.09375 to 0.09375
- image_groups: int32 [8], P('seq'), may hold values 0 or 1
- doc_ids: int32 [8192], replicated, may hold values from 0 to 7, never falling along the last dimension, each value on 1 to 3072 neighbouring positions
Outputs:
- attended: bfloat16 [8192, 2048], P(('seq', 'fsdp'))
Inputs may be any that keep to these rules, and one draw needn't show every extreme that they name: `image_groups`: 1 marks a group of image tokens. `doc_ids`: never falling along the tokens; every document has 1 to 3072 tokens and one has exactly that many.
All inputs are finite; a program needn't handle non-finite values.
Results may differ from a plain program's by a relative error of at most 0.0055.
The roundings to bfloat16 on the way count: a program that leaves them out, or rounds other values in their place, can miss the bound.
Values may be sent and summed in bfloat16 or wider, within the bound.
A program may use at most 128 MiB of HBM per device.

v0:
```python
import functools
import math

import jax
import jax.numpy as jnp
from jax import lax
from jax.experimental import pallas as pl
from jax.experimental.pallas import tpu as pltpu
from jax.sharding import PartitionSpec as P


KVH = 4
HD = 128
QH = 16
SPAN = 3
NEG = -1e30
QUAD = KVH
PER = QH // KVH
WIDE = PER * HD
LINE = 128
MESH = pl.DeviceIdType.MESH


def flip(place, bits):
    out = place
    bit = 1
    while bit <= bits:
        if bits & bit:
            out = out + bit * (1 - 2 * (lax.div(place, bit) % 2))
        bit *= 2
    return out


def gather_kernel(
    seq, fsdp, parts, mod_ref, docs_ref, hidden_ref, w_ref, q_ref,
    kv_out, q_out, limits,
    hid, w, made, mods, q_own, starts, ends,
    local, hid_send, hid_recv, mod_send, mod_recv, q_send, q_recv,
    wz_send, wz_recv, wy_send, wy_recv, kz_send, kz_recv, ky_send, ky_recv, made_sem,
):
    s = lax.axis_index("seq")
    z = lax.axis_index("fsdp")
    h = s % QUAD
    side = lax.div(h, 2)
    carried = lax.div(s, QUAD) % 2
    base = s - h
    twin, across, diag, partner = flip(s, 1), flip(s, 2), flip(s, 3), flip(s, 4)
    ahead, behind = s + QUAD, s - QUAD
    has_ahead, has_behind = ahead < seq, behind >= 0
    step = hidden_ref.shape[0] // parts
    depth = w_ref.shape[1]
    lines = [(way, d) for d in range(1, fsdp) for way in (0, 1)]

    def exists(way, d):
        return z - d >= 0 if way == 0 else z + d <= fsdp - 1

    def source(way, d):
        return z - d if way == 0 else z + d

    def goes_on(way):
        return z + 1 <= fsdp - 1 if way == 0 else z >= 1

    def onward(way):
        return (s, z + 1) if way == 0 else (s, z - 1)

    def columns(head, half):
        return pl.ds(pl.multiple_of((half * KVH + head) * HD, HD), HD)

    def remote(src, dst, send, recv, device):
        return pltpu.make_async_remote_copy(
            src_ref=src, dst_ref=dst, send_sem=send, recv_sem=recv, device_id=device, device_id_type=MESH
        )

    keep = [pltpu.make_async_copy(hidden_ref, hid.at[h], local.at[0])]
    for m in range(2):
        for half in range(2):
            keep.append(
                pltpu.make_async_copy(
                    w_ref.at[m, :, columns(h, half)],
                    w.at[z, m, :, half * HD : (half + 1) * HD],
                    local.at[1 + 2 * m + half],
                )
            )
    q_in = pltpu.make_async_copy(q_ref.at[:, pl.ds(pl.multiple_of(h * WIDE, HD), WIDE)], q_own, local.at[5])
    q_keep = pltpu.make_async_copy(q_own, q_out.at[0], local.at[6])
    mod_in = pltpu.make_async_copy(mod_ref, mods.at[h], local.at[7])
    for copy in keep:
        copy.start()
    q_in.start()
    mod_in.start()

    barrier = pltpu.get_barrier_semaphore()
    near = [(twin, z), (across, z), (diag, z), (partner, z)]
    near += [((s + QUAD) % seq, z), ((s - QUAD + seq) % seq, z)]
    for device in near:
        pl.semaphore_signal(barrier, inc=1, device_id=device, device_id_type=MESH)
    for way in (0, 1):
        @pl.when(goes_on(way))
        def _(way=way):
            pl.semaphore_signal(barrier, inc=1, device_id=onward(way), device_id_type=MESH)
    both = (z >= 1).astype(jnp.int32) + (z <= fsdp - 2).astype(jnp.int32)
    pl.semaphore_wait(barrier, len(near) + both)

    def w_slot(zs, m, half):
        return w.at[zs, m, :, half * HD : (half + 1) * HD]

    def w_line(way, d, half):
        src = w_ref.at[carried, :, columns(h, half)] if d == 0 else w_slot(source(way, d), carried, half)
        zs = z if d == 0 else source(way, d)
        return remote(
            src, w_slot(zs, carried, half), wz_send.at[way, d, half], wz_recv.at[way, d + 1, half], onward(way)
        )

    def w_arrived(way, d, half):
        return remote(
            w_slot(source(way, d), carried, half), w_slot(source(way, d), carried, half),
            wz_send.at[way, d, half], wz_recv.at[way, d, half], (s, z),
        )

    def w_swap(way, d, half):
        slot = w_slot(source(way, d), carried, half)
        return remote(slot, slot, wy_send.at[way, d, half], wy_recv.at[way, d, half], (partner, z))

    def w_swapped(way, d, half):
        slot = w_slot(source(way, d), 1 - carried, half)
        return remote(slot, slot, wy_send.at[way, d, half], wy_recv.at[way, d, half], (partner, z))

    def rows(part):
        return slice(part * step, (part + 1) * step)

    def hid_to(which, device, part):
        return remote(
            hidden_ref.at[rows(part)], hid.at[h, rows(part)],
            hid_send.at[which, part], hid_recv.at[which, part], (device, z),
        )

    def hid_relay(part):
        slot = hid.at[across - base, rows(part)]
        return remote(slot, slot, hid_send.at[2, part], hid_recv.at[2, part], (twin, z))

    def hid_got(which, device, part):
        slot = hid.at[device - base, rows(part)]
        return remote(slot, slot, hid_send.at[which, part], hid_recv.at[which, part], (twin, z))

    mates = (twin, across, diag)

    def mod_to(i):
        return remote(mod_ref, mods.at[h], mod_send.at[i], mod_recv.at[i], (mates[i], z))

    def mod_got(i):
        slot = mods.at[mates[i] - base]
        return remote(slot, slot, mod_send.at[i], mod_recv.at[i], (mates[i], z))

    def q_to(i):
        head = mates[i] - base
        return remote(
            q_ref.at[:, pl.ds(pl.multiple_of(head * WIDE, HD), WIDE)], q_out.at[1 + i],
            q_send.at[i], q_recv.at[i], (mates[i], z),
        )

    def q_got(i):
        slot = q_out.at[1 + i]
        return remote(slot, slot, q_send.at[i], q_recv.at[i], (mates[i], z))

    def first_group(unit):
        return 2 * side if unit == 0 else 2 - 2 * side

    def kv_slot(unit, zs):
        return kv_out.at[:, pl.ds(SPAN + first_group(unit), 2), zs]

    def kv_line(unit, way, d):
        src = made.at[unit] if d == 0 else kv_slot(unit, source(way, d))
        zs = z if d == 0 else source(way, d)
        return remote(
            src, kv_slot(unit, zs), kz_send.at[unit, way, d], kz_recv.at[unit, way, d + 1], onward(way)
        )

    def kv_arrived(unit, way, d):
        slot = kv_slot(unit, source(way, d))
        return remote(slot, slot, kz_send.at[unit, way, d], kz_recv.at[unit, way, d], (s, z))

    def ahead_index(way, d):
        return 0 if d == 0 else 1 + 2 * (d - 1) + way

    def kv_ahead(unit, way, d, i):
        group = first_group(unit) + i
        zs = z if d == 0 else source(way, d)
        src = made.at[unit, :, pl.ds(i, 1)] if d == 0 else kv_out.at[:, pl.ds(SPAN + group, 1), zs]
        at = ahead_index(way, d)
        return remote(
            src, kv_out.at[:, pl.ds(group - 1, 1), zs],
            ky_send.at[unit, at, i], ky_recv.at[unit, at, i], (ahead, z),
        )

    def kv_behind(unit, way, d, i):
        group = first_group(unit) + i
        zs = z if d == 0 else source(way, d)
        slot = kv_out.at[:, pl.ds(group - 1, 1), zs]
        at = ahead_index(way, d)
        return remote(slot, slot, ky_send.at[unit, at, i], ky_recv.at[unit, at, i], (ahead, z))

    def kv_keep(unit):
        return pltpu.make_async_copy(made.at[unit], kv_slot(unit, z), made_sem.at[unit])

    def when(holds, act):
        @pl.when(holds)
        def _():
            act()

    for half in range(2):
        for way in (0, 1):
            when(goes_on(way), lambda: w_line(way, 0, half).start())
    for i in range(3):
        mod_to(i).start()
    for part in range(parts):
        hid_to(1, across, part).start()
    for part in range(parts):
        hid_to(0, twin, part).start()
    for i in (1, 2, 0):
        q_to(i).start()

    def pass_weights(way, d, half):
        def act():
            w_arrived(way, d, half).wait_recv()
            if d < fsdp - 1:
                when(goes_on(way), lambda: w_line(way, d, half).start())
            w_swap(way, d, half).start()

        when(exists(way, d), act)

    def pass_hidden(part):
        hid_got(1, across, part).wait_recv()
        hid_relay(part).start()

    def send_ahead(unit, way, d):
        for i in range(2):
            when(
                jnp.logical_and(has_ahead, first_group(unit) + i >= 1),
                lambda: kv_ahead(unit, way, d, i).start(),
            )

    def pass_kv(unit, way, d):
        def act():
            kv_arrived(unit, way, d).wait_recv()
            if d < fsdp - 1:
                when(goes_on(way), lambda: kv_line(unit, way, d).start())
            send_ahead(unit, way, d)

        when(exists(way, d), act)

    def project(unit):
        for i in range(2):
            group = first_group(unit) + i
            image = jnp.max(mods[group]) == 1
            total = None
            for zs in range(fsdp):
                weight = jnp.where(image, w[zs, 1], w[zs, 0])
                term = jnp.dot(
                    hid[group, :, zs * depth : (zs + 1) * depth], weight, preferred_element_type=jnp.float32
                )
                total = term if total is None else total + term
            rounded = total.astype(jnp.bfloat16)
            made[unit, 0, i] = rounded[:, :HD]
            made[unit, 1, i] = rounded[:, HD:]

    def send_made(unit):
        for way in (0, 1):
            when(goes_on(way), lambda: kv_line(unit, way, 0).start())
        send_ahead(unit, 0, 0)
        kv_keep(unit).start()

    starts[...], ends[...] = bounds(docs_ref[...])
    mod_in.wait()
    for i in range(3):
        mod_got(i).wait_recv()
    block = hidden_ref.shape[0] * fsdp
    origin = (base - SPAN) * block
    for slot in range(QUAD):
        group = flip(s, slot)
        image = mods[group - base, :1] == 1
        for i in range(hidden_ref.shape[0] // LINE):
            first = group * block + z * hidden_ref.shape[0] + i * LINE
            line = lax.div(first, LINE)
            at = slice(i * LINE, (i + 1) * LINE)
            place = first + lax.broadcasted_iota(jnp.int32, (1, LINE), 1)
            last = jnp.minimum(ends[pl.ds(line, 1), :], group * block + block - 1)
            limits[slot : slot + 1, at] = starts[pl.ds(line, 1), :] - origin
            limits[QUAD + slot : QUAD + slot + 1, at] = jnp.where(image, last, place) - origin

    done = 0
    for d in range(1, fsdp):
        for half in range(2):
            for way in (0, 1):
                pass_weights(way, d, half)
        if done < parts - 2:
            pass_hidden(done)
            done += 1
    for copy in keep:
        copy.wait()
    for part in range(parts):
        hid_got(0, twin, part).wait_recv()
    for way, d in lines:
        for half in range(2):
            when(exists(way, d), lambda: w_swapped(way, d, half).wait_recv())
    project(0)
    q_in.wait()
    q_keep.start()
    send_made(0)
    while done < parts:
        pass_hidden(done)
        done += 1
    for way in (0, 1):
        pass_kv(0, way, 1)
    for part in range(parts):
        hid_got(2, diag, part).wait_recv()
    project(1)
    for way in (0, 1):
        pass_kv(0, way, 2)
    send_made(1)
    for d in range(3, fsdp):
        for way in (0, 1):
            pass_kv(0, way, d)
    for d in range(1, fsdp):
        for way in (0, 1):
            pass_kv(1, way, d)
    for i in range(3):
        q_got(i).wait_recv()
    for unit in range(2):
        for way, d in [(0, 0)] + lines:
            for i in range(2):
                holds = jnp.logical_and(has_behind, first_group(unit) + i >= 1)
                if d:
                    holds = jnp.logical_and(holds, exists(way, d))
                when(holds, lambda: kv_behind(unit, way, d, i).wait_recv())

    q_keep.wait()
    for unit in range(2):
        kv_keep(unit).wait()
    for half in range(2):
        for way in (0, 1):
            when(goes_on(way), lambda: w_line(way, 0, half).wait_send())
            for d in range(1, fsdp):
                def act(way=way, d=d, half=half):
                    if d < fsdp - 1:
                        when(goes_on(way), lambda: w_line(way, d, half).wait_send())
                    w_swap(way, d, half).wait_send()

                when(exists(way, d), act)
    for i in range(3):
        mod_to(i).wait_send()
        q_to(i).wait_send()
    for part in range(parts):
        hid_to(0, twin, part).wait_send()
        hid_to(1, across, part).wait_send()
        hid_relay(part).wait_send()

    def sent_ahead(unit, way, d):
        for i in range(2):
            when(
                jnp.logical_and(has_ahead, first_group(unit) + i >= 1),
                lambda: kv_ahead(unit, way, d, i).wait_send(),
            )

    for unit in range(2):
        for way in (0, 1):
            when(goes_on(way), lambda: kv_line(unit, way, 0).wait_send())
        sent_ahead(unit, 0, 0)
        for way, d in lines:
            def act(unit=unit, way=way, d=d):
                if d < fsdp - 1:
                    when(goes_on(way), lambda: kv_line(unit, way, d).wait_send())
                sent_ahead(unit, way, d)

            when(exists(way, d), act)


def shifted(x, by, axis, fill):
    size = x.shape[axis]
    place = lax.broadcasted_iota(jnp.int32, x.shape, axis)
    moved = pltpu.roll(x, by % size, axis)
    inside = place >= by if by > 0 else place < size + by
    return jnp.where(inside, moved, fill)


def spread(x, pick, sign, fill):
    by = 1
    while by < x.shape[1]:
        x = pick(x, shifted(x, sign * by, 1, fill))
        by *= 2
    edge = x[:, -1:] if sign > 0 else x[:, :1]
    rows = shifted(jnp.broadcast_to(edge, x.shape), sign, 0, fill)
    by = 1
    while by < x.shape[0]:
        rows = pick(rows, shifted(rows, sign * by, 0, fill))
        by *= 2
    return pick(x, rows)


def bounds(docs):
    count = docs.shape[0] * docs.shape[1]
    place = (
        lax.broadcasted_iota(jnp.int32, docs.shape, 0) * docs.shape[1]
        + lax.broadcasted_iota(jnp.int32, docs.shape, 1)
    )
    lane = lax.broadcasted_iota(jnp.int32, docs.shape, 1)
    width = docs.shape[1]
    turned = pltpu.roll(docs, 1, 1)
    before = jnp.where(lane == 0, shifted(turned, 1, 0, -1), turned)
    turned = pltpu.roll(docs, width - 1, 1)
    after = jnp.where(lane == width - 1, shifted(turned, -1, 0, -1), turned)
    starts = jnp.where(docs != before, place, 0)
    ends = jnp.where(docs != after, place, count - 1)
    return spread(starts, jnp.maximum, 1, 0), spread(ends, jnp.minimum, -1, count - 1)


def gather(hidden, queries, kv_weights, image_groups, doc_ids):
    seq, fsdp = lax.axis_size("seq"), lax.axis_size("fsdp")
    rows, width = hidden.shape
    depth = kv_weights.shape[1]
    parts = 4
    marked = jnp.broadcast_to(image_groups[0], (8, LINE))
    docs = doc_ids.reshape(-1, LINE)
    anywhere = pl.BlockSpec(memory_space=pl.ANY)
    far = pl.BlockSpec(memory_space=pltpu.HBM)
    vmem = pl.BlockSpec(memory_space=pltpu.VMEM)
    dma = pltpu.SemaphoreType.DMA
    bf16 = jnp.bfloat16
    return pl.pallas_call(
        functools.partial(gather_kernel, seq, fsdp, parts),
        in_specs=[far, vmem, far, far, far],
        out_specs=[anywhere, anywhere, vmem],
        out_shape=[
            jax.ShapeDtypeStruct((2, SPAN + QUAD, fsdp, rows, HD), bf16),
            jax.ShapeDtypeStruct((QUAD, rows, WIDE), bf16),
            jax.ShapeDtypeStruct((2 * QUAD, rows), jnp.int32),
        ],
        scratch_shapes=[
            pltpu.VMEM((QUAD, rows, width), bf16),
            pltpu.VMEM((fsdp, 2, depth, 2 * HD), bf16),
            pltpu.VMEM((2, 2, 2, rows, HD), bf16),
            pltpu.VMEM((QUAD, 8, LINE), jnp.int32),
            pltpu.VMEM((rows, WIDE), bf16),
            pltpu.VMEM(docs.shape, jnp.int32),
            pltpu.VMEM(docs.shape, jnp.int32),
            dma((8,)),
            dma((3, parts)),
            dma((3, parts)),
            dma((3,)),
            dma((3,)),
            dma((3,)),
            dma((3,)),
            dma((2, fsdp, 2)),
            dma((2, fsdp + 1, 2)),
            dma((2, fsdp, 2)),
            dma((2, fsdp, 2)),
            dma((2, 2, fsdp)),
            dma((2, 2, fsdp + 1)),
            dma((2, 2 * fsdp, 2)),
            dma((2, 2 * fsdp, 2)),
            dma((2,)),
        ],
        compiler_params=pltpu.CompilerParams(
            collective_id=0, has_side_effects=True, vmem_limit_bytes=32 * 1024 * 1024
        ),
        name="gather",
    )(marked, docs, *(pltpu.with_memory_space_constraint(x, pltpu.HBM) for x in (hidden, kv_weights, queries)))


def attend_kernel(key_block, slot, limits_ref, q_ref, k_ref, after_ref, out_ref, qt, top, total, acc):
    rows = q_ref.shape[1]
    lo_ref = limits_ref.at[slot : slot + 1]
    hi_ref = limits_ref.at[QUAD + slot : QUAD + slot + 1]
    lo, hi = lo_ref[...], hi_ref[...]
    lo_min, lo_max, hi_min, hi_max = jnp.min(lo), jnp.max(lo), jnp.min(hi), jnp.max(hi)
    first = lax.div(lo_min, key_block)
    end = lax.div(hi_max, key_block) + 1
    full_first = jnp.minimum(lax.div(lo_max + key_block - 1, key_block), end)
    full_end = jnp.maximum(lax.div(hi_min + 1, key_block), full_first)

    lanes = [slice(g * rows, (g + 1) * rows) for g in range(PER)]
    factor = math.log2(math.e) / math.sqrt(HD)
    for g in range(PER):
        qt[:, g * rows : (g + 1) * rows] = q_ref[slot, :, g * HD : (g + 1) * HD].T
    top[...] = jnp.full_like(top, NEG)
    total[...] = jnp.zeros_like(total)
    acc[...] = jnp.zeros_like(acc)

    def step(masked, b, _):
        at = pl.multiple_of(b * key_block, key_block)
        keys = k_ref[0, pl.ds(at, key_block), :]
        values = k_ref[1, pl.ds(at, key_block), :]
        if masked:
            place = at + lax.broadcasted_iota(jnp.int32, (key_block, rows), 0)
            allowed = jnp.logical_and(place >= lo_ref[...], place <= hi_ref[...])
        scores = [jnp.dot(keys, qt[:, at_g], preferred_element_type=jnp.float32) for at_g in lanes]
        if masked:
            scores = [jnp.where(allowed, score, NEG) for score in scores]
        before = [top[:, at_g] for at_g in lanes]
        peak = [
            jnp.maximum(old, jnp.max(score, axis=0, keepdims=True))
            for old, score in zip(before, scores)
        ]
        weights = [jnp.exp2((score - high) * factor) for score, high in zip(scores, peak)]
        shrink = [jnp.exp2((old - high) * factor) for old, high in zip(before, peak)]
        added = [jnp.sum(weight, axis=0, keepdims=True) for weight in weights]
        mixed = [
            lax.dot_general(
                values,
                weight.astype(jnp.bfloat16),
                (((0,), (0,)), ((), ())),
                preferred_element_type=jnp.float32,
            )
            for weight in weights
        ]
        for g, at_g in enumerate(lanes):
            top[:, at_g] = peak[g]
            total[:, at_g] = total[:, at_g] * shrink[g] + added[g]
            acc[:, at_g] = acc[:, at_g] * shrink[g] + mixed[g]
        return 0

    lax.fori_loop(first, full_first, functools.partial(step, True), 0)
    lax.fori_loop(full_first, full_end, functools.partial(step, False), 0)
    lax.fori_loop(full_end, end, functools.partial(step, True), 0)
    for g in range(PER):
        mixed = (acc[:, lanes[g]] / total[:, lanes[g]]).T
        out_ref[:, g * HD : (g + 1) * HD] = mixed.astype(out_ref.dtype)


def attend(kv, queries, limits, after, slot):
    fsdp = lax.axis_size("fsdp")
    _, rows, wide = queries.shape
    n_keys = kv.shape[1] * kv.shape[2] * kv.shape[3]
    kv = kv.reshape(2, n_keys, HD)
    key_block = math.gcd(rows * fsdp, 512)
    vmem = pl.BlockSpec(memory_space=pltpu.VMEM)
    work = rows * PER * n_keys // 4
    return pl.pallas_call(
        functools.partial(attend_kernel, key_block, slot),
        in_specs=[vmem] * 3 + [pl.BlockSpec(memory_space=pl.ANY)],
        out_specs=vmem,
        out_shape=jax.ShapeDtypeStruct((rows, wide), queries.dtype),
        scratch_shapes=[
            pltpu.VMEM((HD, PER * rows), jnp.bfloat16),
            pltpu.VMEM((1, PER * rows), jnp.float32),
            pltpu.VMEM((1, PER * rows), jnp.float32),
            pltpu.VMEM((HD, PER * rows), jnp.float32),
        ],
        compiler_params=pltpu.CompilerParams(vmem_limit_bytes=16 * 1024 * 1024),
        cost_estimate=pl.CostEstimate(flops=4 * HD * work, bytes_accessed=4 * HD * n_keys, transcendentals=work),
    )(limits, queries, kv, after)


def assemble_kernel(*refs):
    h = lax.axis_index("seq") % QUAD
    out_ref, sems = refs[QUAD:]
    wide = refs[0].shape[1]
    copies = [
        pltpu.make_async_copy(
            refs[slot], out_ref.at[:, pl.ds(pl.multiple_of(flip(h, slot) * wide, HD), wide)], sems.at[slot]
        )
        for slot in range(QUAD)
    ]
    for copy in copies:
        copy.start()
    for copy in copies:
        copy.wait()


def assemble(pieces):
    rows, wide = pieces[0].shape
    return pl.pallas_call(
        assemble_kernel,
        in_specs=[pl.BlockSpec(memory_space=pltpu.VMEM)] * QUAD,
        out_specs=pl.BlockSpec(memory_space=pl.ANY),
        out_shape=jax.ShapeDtypeStruct((rows, QUAD * wide), pieces[0].dtype),
        scratch_shapes=[pltpu.SemaphoreType.DMA((QUAD,))],
        compiler_params=pltpu.CompilerParams(vmem_limit_bytes=8 * 1024 * 1024),
        name="assemble",
    )(*pieces)


def local(hidden, queries, kv_weights, image_groups, doc_ids):
    seq = lax.axis_size("seq")
    kv, q, limits = gather(hidden, queries, kv_weights, image_groups, doc_ids)
    pieces = [None] * QUAD
    mixed = limits
    for slot in (3, 2, 1, 0):
        mixed = attend(kv, q, limits, mixed, slot)
        swap = [(i, i ^ slot) for i in range(seq)]
        pieces[slot] = lax.ppermute(mixed, "seq", swap) if slot else mixed
    return assemble(pieces)


def solution(mesh):
    in_specs = (
        P(("seq", "fsdp"), None),
        P(("seq", "fsdp"), None),
        P(None, "fsdp", None),
        P("seq"),
        P(),
    )
    out_specs = P(("seq", "fsdp"), None)
    return jax.shard_map(local, mesh=mesh, in_specs=in_specs, out_specs=out_specs, check_vma=False)
```

profile of v0, /device:TPU:5, one launch (start us, length us, event | category | flops | bytes accessed | tf_op | source)
XLA Modules:
  0.0 113.4 jit_solution(759564424591767641)
XLA Ops:
  0.7 0.0 copy-start
  0.7 0.7 copy-done
  1.4 80.5 %gather.1 = (bf16[2,7,4,256,128]{4,3,2,1,0:T(8,128)(2,1)S(1)}, bf16[4,256,512]{2,1,0:T(8,128)(2,1)S(1)}, s32[8,256]{1,0:T(8,128)S(1)}) custom-call(s32[8,128]{1,0:T(8,128)S(1)} %broadcast_in_dim.3.mod_ref, s32[64,128]{1,0:T(8,128)S(1)} %bitcast.8, bf16[256,3584]{1,0:T(8,128)(2,1)} %hidden_ref.1, bf16[2,896,1024]{2,1,0:T(8,128)(2,1)} %w_ref.1, ...), custom_call_target="tpu_custom_call" | custom-call | tf_op jit(solution)/shard_map/gather/pallas_call | solution.py:428
  81.9 2.5 %shard_map.55.after_ref = bf16[256,512]{1,0:T(8,128)(2,1)S(1)} custom-call(s32[8,256]{1,0:T(8,128)S(1)} %get-tuple-element.8.limits_ref.after_ref, bf16[4,256,512]{2,1,0:T(8,128)(2,1)S(1)} %get-tuple-element.9.q_ref, bf16[2,7168,128]{2,1,0:T(8,128)(2,1)S(1)} %bitcast.4, s32[8,256]{1,0:T(8,128)S(1)} %get-tuple-element.8.limits_ref.after_ref), custom_call_target="tpu_custom_call" | custom-call | flops 939524096 | bytes 3670016 | tf_op jit(solution)/shard_map/pallas_call | solution.py:537
  84.4 3.5 %shard_map.56.after_ref = bf16[256,512]{1,0:T(8,128)(2,1)S(1)} custom-call(s32[8,256]{1,0:T(8,128)S(1)} %get-tuple-element.8.limits_ref.after_ref, bf16[4,256,512]{2,1,0:T(8,128)(2,1)S(1)} %get-tuple-element.9.q_ref, bf16[2,7168,128]{2,1,0:T(8,128)(2,1)S(1)} %bitcast.5, bf16[256,512]{1,0:T(8,128)(2,1)S(1)} %shard_map.55.after_ref), custom_call_target="tpu_custom_call" | custom-call | flops 939524096 | bytes 3670016 | tf_op jit(solution)/shard_map/pallas_call | solution.py:537
  88.0 3.7 %shard_map.57.after_ref = bf16[256,512]{1,0:T(8,128)(2,1)S(1)} custom-call(s32[8,256]{1,0:T(8,128)S(1)} %get-tuple-element.8.limits_ref.after_ref, bf16[4,256,512]{2,1,0:T(8,128)(2,1)S(1)} %get-tuple-element.9.q_ref, bf16[2,7168,128]{2,1,0:T(8,128)(2,1)S(1)} %bitcast.6, bf16[256,512]{1,0:T(8,128)(2,1)S(1)} %shard_map.56.after_ref), custom_call_target="tpu_custom_call" | custom-call | flops 939524096 | bytes 3670016 | tf_op jit(solution)/shard_map/pallas_call | solution.py:537
  91.7 7.0 %collective-permute-start = (bf16[256,512]{1,0:T(8,128)(2,1)S(1)}, bf16[256,512]{1,0:T(8,128)(2,1)S(1)}, u32[]{:S(2)}, u32[]{:S(2)}) collective-permute-start(bf16[256,512]{1,0:T(8,128)(2,1)S(1)} %shard_map.57.after_ref), channel_id=1, source_target_pairs={{0,4},{4,0},{8,12},{12,8},{16,20},{20,16},{24,28},{28,24},{1,5},{5... | collective-permute-start | bytes 786440 | tf_op jit(solution)/shard_map/ppermute | solution.py:590
  98.6 0.0 collective-permute-start.1
  98.6 1.7 %collective-permute-start.2 = (bf16[256,512]{1,0:T(8,128)(2,1)S(1)}, bf16[256,512]{1,0:T(8,128)(2,1)S(1)}, u32[]{:S(2)}, u32[]{:S(2)}) collective-permute-start(bf16[256,512]{1,0:T(8,128)(2,1)S(1)} %shard_map.55.after_ref), channel_id=1, source_target_pairs={{0,12},{4,8},{8,4},{12,0},{16,28},{20,24},{24,20},{28,16},{1,13},{... | collective-permute-start | bytes 786440 | tf_op jit(solution)/shard_map/ppermute | solution.py:590
  100.3 5.6 %shard_map.58.refs_0_ = bf16[256,512]{1,0:T(8,128)(2,1)S(1)} custom-call(s32[8,256]{1,0:T(8,128)S(1)} %get-tuple-element.8.limits_ref.after_ref, bf16[4,256,512]{2,1,0:T(8,128)(2,1)S(1)} %get-tuple-element.9.q_ref, bf16[2,7168,128]{2,1,0:T(8,128)(2,1)S(1)} %bitcast.7, bf16[256,512]{1,0:T(8,128)(2,1)S(1)} %shard_map.57.after_ref), custom_call_target="tpu_custom_call" | custom-call | flops 939524096 | bytes 3670016 | tf_op jit(solution)/shard_map/pallas_call | solution.py:537
  105.9 0.0 collective-permute-done.refs_1_
  105.9 0.5 collective-permute-done.1.refs_2_
  106.4 5.9 %collective-permute-done.2.refs_3_ = bf16[256,512]{1,0:T(8,128)(2,1)S(1)} collective-permute-done((bf16[256,512]{1,0:T(8,128)(2,1)S(1)}, bf16[256,512]{1,0:T(8,128)(2,1)S(1)}, u32[]{:S(2)}, u32[]{:S(2)}) %collective-permute-start.2) | collective-permute-done | bytes 262176 | tf_op jit(solution)/shard_map/ppermute | solution.py:590
  112.3 1.0 assemble.1
  (1 shorter events, 0.0 us)
Async XLA Ops:
  0.7 0.8 copy-start
  91.7 14.2 %collective-permute-start = (bf16[256,512]{1,0:T(8,128)(2,1)S(1)}, bf16[256,512]{1,0:T(8,128)(2,1)S(1)}, u32[]{:S(2)}, u32[]{:S(2)}) collective-permute-start(bf16[256,512]{1,0:T(8,128)(2,1)S(1)} %shard_map.57.after_ref), channel_id=1, source_target_pairs={{0,4},{4,0},{8,12},{12,8},{16,20},{20,16},{24,28},{28,24},{1,5},{5... | collective-permute-start | bytes 786440 | tf_op jit(solution)/shard_map/ppermute | solution.py:590
  98.6 7.8 %collective-permute-start.1 = (bf16[256,512]{1,0:T(8,128)(2,1)S(1)}, bf16[256,512]{1,0:T(8,128)(2,1)S(1)}, u32[]{:S(2)}, u32[]{:S(2)}) collective-permute-start(bf16[256,512]{1,0:T(8,128)(2,1)S(1)} %shard_map.56.after_ref), channel_id=1, source_target_pairs={{0,8},{4,12},{8,0},{12,4},{16,24},{20,28},{24,16},{28,20},{1,9},{5... | collective-permute-start | bytes 786440 | tf_op jit(solution)/shard_map/ppermute | solution.py:590
  98.6 13.6 %collective-permute-start.2 = (bf16[256,512]{1,0:T(8,128)(2,1)S(1)}, bf16[256,512]{1,0:T(8,128)(2,1)S(1)}, u32[]{:S(2)}, u32[]{:S(2)}) collective-permute-start(bf16[256,512]{1,0:T(8,128)(2,1)S(1)} %shard_map.55.after_ref), channel_id=1, source_target_pairs={{0,12},{4,8},{8,4},{12,0},{16,28},{20,24},{24,20},{28,16},{1,13},{... | collective-permute-start | bytes 786440 | tf_op jit(solution)/shard_map/ppermute | solution.py:590
where the time goes:
time: 114 us; the launch traced here: 113 us
  Pallas kernels  96.8 us (85%)
  starting transfers between devices  8.68 us (8%)
  waiting for transfers between devices  6.37 us (6%)
    pallas_call x1, Pallas kernels, gather(): pl.pallas_call(functools.partial(gather_kernel, seq, fsdp, parts), in_spe...  80.5 us
    pallas_call x4, Pallas kernels, attend(): pl.pallas_call(functools.partial(attend_kernel, key_block, slot), in_spec...  15.3 us
    ppermute x3, starting transfers between devices, local(): pieces[slot] = lax.ppermute(mixed, 'seq', swap) if slot else mixed  8.68 us
    ppermute x3, waiting for transfers between devices, local(): pieces[slot] = lax.ppermute(mixed, 'seq', swap) if slot else mixed  6.37 us
  transfers between devices with their start and end apart: 3, of which 2 were waited for; matrix products, arithmetic and copies ran while one was open for 0% of the time, Pallas kernels for 5%

commit v1 on v0

--- a/solution.py
+++ b/solution.py
@@ -34,14 +34,13 @@
 def gather_kernel(
     seq, fsdp, parts, mod_ref, docs_ref, hidden_ref, w_ref, q_ref,
     kv_out, q_out, limits,
-    hid, w, made, mods, q_own, starts, ends,
+    hid, w, made, mods, q_own, docs, starts, ends,
     local, hid_send, hid_recv, mod_send, mod_recv, q_send, q_recv,
     wz_send, wz_recv, wy_send, wy_recv, kz_send, kz_recv, ky_send, ky_recv, made_sem,
 ):
     s = lax.axis_index("seq")
     z = lax.axis_index("fsdp")
     h = s % QUAD
-    side = lax.div(h, 2)
     carried = lax.div(s, QUAD) % 2
     base = s - h
     twin, across, diag, partner = flip(s, 1), flip(s, 2), flip(s, 3), flip(s, 4)
@@ -84,6 +83,8 @@
     q_in = pltpu.make_async_copy(q_ref.at[:, pl.ds(pl.multiple_of(h * WIDE, HD), WIDE)], q_own, local.at[5])
     q_keep = pltpu.make_async_copy(q_own, q_out.at[0], local.at[6])
     mod_in = pltpu.make_async_copy(mod_ref, mods.at[h], local.at[7])
+    docs_in = pltpu.make_async_copy(docs_ref, docs, local.at[8])
+    docs_in.start()
     for copy in keep:
         copy.start()
     q_in.start()
@@ -162,11 +163,10 @@
         slot = q_out.at[1 + i]
         return remote(slot, slot, q_send.at[i], q_recv.at[i], (mates[i], z))
 
-    def first_group(unit):
-        return 2 * side if unit == 0 else 2 - 2 * side
+    groups = [flip(s, unit) - base for unit in range(QUAD)]
 
     def kv_slot(unit, zs):
-        return kv_out.at[:, pl.ds(SPAN + first_group(unit), 2), zs]
+        return kv_out.at[:, SPAN + groups[unit], zs]
 
     def kv_line(unit, way, d):
         src = made.at[unit] if d == 0 else kv_slot(unit, source(way, d))
@@ -182,22 +182,19 @@
     def ahead_index(way, d):
         return 0 if d == 0 else 1 + 2 * (d - 1) + way
 
-    def kv_ahead(unit, way, d, i):
-        group = first_group(unit) + i
+    def kv_ahead(unit, way, d):
         zs = z if d == 0 else source(way, d)
-        src = made.at[unit, :, pl.ds(i, 1)] if d == 0 else kv_out.at[:, pl.ds(SPAN + group, 1), zs]
+        src = made.at[unit] if d == 0 else kv_slot(unit, zs)
         at = ahead_index(way, d)
         return remote(
-            src, kv_out.at[:, pl.ds(group - 1, 1), zs],
-            ky_send.at[unit, at, i], ky_recv.at[unit, at, i], (ahead, z),
-        )
-
-    def kv_behind(unit, way, d, i):
-        group = first_group(unit) + i
+            src, kv_out.at[:, groups[unit] - 1, zs], ky_send.at[unit, at], ky_recv.at[unit, at], (ahead, z)
+        )
+
+    def kv_behind(unit, way, d):
         zs = z if d == 0 else source(way, d)
-        slot = kv_out.at[:, pl.ds(group - 1, 1), zs]
+        slot = kv_out.at[:, groups[unit] - 1, zs]
         at = ahead_index(way, d)
-        return remote(slot, slot, ky_send.at[unit, at, i], ky_recv.at[unit, at, i], (ahead, z))
+        return remote(slot, slot, ky_send.at[unit, at], ky_recv.at[unit, at], (ahead, z))
 
     def kv_keep(unit):
         return pltpu.make_async_copy(made.at[unit], kv_slot(unit, z), made_sem.at[unit])
@@ -233,11 +230,7 @@
         hid_relay(part).start()
 
     def send_ahead(unit, way, d):
-        for i in range(2):
-            when(
-                jnp.logical_and(has_ahead, first_group(unit) + i >= 1),
-                lambda: kv_ahead(unit, way, d, i).start(),
-            )
+        when(jnp.logical_and(has_ahead, groups[unit] >= 1), lambda: kv_ahead(unit, way, d).start())
 
     def pass_kv(unit, way, d):
         def act():
@@ -249,19 +242,17 @@
         when(exists(way, d), act)
 
     def project(unit):
-        for i in range(2):
-            group = first_group(unit) + i
-            image = jnp.max(mods[group]) == 1
-            total = None
-            for zs in range(fsdp):
-                weight = jnp.where(image, w[zs, 1], w[zs, 0])
-                term = jnp.dot(
-                    hid[group, :, zs * depth : (zs + 1) * depth], weight, preferred_element_type=jnp.float32
-                )
-                total = term if total is None else total + term
-            rounded = total.astype(jnp.bfloat16)
-            made[unit, 0, i] = rounded[:, :HD]
-            made[unit, 1, i] = rounded[:, HD:]
+        group = groups[unit]
+        image = jnp.max(mods[group]) == 1
+        total = None
+        for zs in range(fsdp):
+            weight = jnp.where(image, w[zs, 1], w[zs, 0])
+            rows_at = hid[group, :, zs * depth : (zs + 1) * depth]
+            term = jnp.dot(rows_at, weight, preferred_element_type=jnp.float32)
+            total = term if total is None else total + term
+        rounded = total.astype(jnp.bfloat16)
+        made[unit, 0] = rounded[:, :HD]
+        made[unit, 1] = rounded[:, HD:]
 
     def send_made(unit):
         for way in (0, 1):
@@ -269,7 +260,8 @@
         send_ahead(unit, 0, 0)
         kv_keep(unit).start()
 
-    starts[...], ends[...] = bounds(docs_ref[...])
+    docs_in.wait()
+    starts[...], ends[...] = bounds(docs[...])
     mod_in.wait()
     for i in range(3):
         mod_got(i).wait_recv()
@@ -305,36 +297,43 @@
     project(0)
     q_in.wait()
     q_keep.start()
+    project(1)
     send_made(0)
-    while done < parts:
-        pass_hidden(done)
-        done += 1
-    for way in (0, 1):
-        pass_kv(0, way, 1)
+    send_made(1)
+
+    def relay(unit, d):
+        for way in (0, 1):
+            pass_kv(unit, way, d)
+
+    pass_hidden(parts - 2)
+    relay(0, 1)
+    relay(1, 1)
+    pass_hidden(parts - 1)
+    relay(0, 2)
     for part in range(parts):
         hid_got(2, diag, part).wait_recv()
-    project(1)
-    for way in (0, 1):
-        pass_kv(0, way, 2)
-    send_made(1)
+    project(2)
+    relay(1, 2)
+    project(3)
+    send_made(2)
+    send_made(3)
     for d in range(3, fsdp):
-        for way in (0, 1):
-            pass_kv(0, way, d)
+        relay(0, d)
+        relay(1, d)
     for d in range(1, fsdp):
-        for way in (0, 1):
-            pass_kv(1, way, d)
+        relay(2, d)
+        relay(3, d)
     for i in range(3):
         q_got(i).wait_recv()
-    for unit in range(2):
+    for unit in range(QUAD):
         for way, d in [(0, 0)] + lines:
-            for i in range(2):
-                holds = jnp.logical_and(has_behind, first_group(unit) + i >= 1)
-                if d:
-                    holds = jnp.logical_and(holds, exists(way, d))
-                when(holds, lambda: kv_behind(unit, way, d, i).wait_recv())
+            holds = jnp.logical_and(has_behind, groups[unit] >= 1)
+            if d:
+                holds = jnp.logical_and(holds, exists(way, d))
+            when(holds, lambda: kv_behind(unit, way, d).wait_recv())
 
     q_keep.wait()
-    for unit in range(2):
+    for unit in range(QUAD):
         kv_keep(unit).wait()
     for half in range(2):
         for way in (0, 1):
@@ -355,13 +354,9 @@
         hid_relay(part).wait_send()
 
     def sent_ahead(unit, way, d):
-        for i in range(2):
-            when(
-                jnp.logical_and(has_ahead, first_group(unit) + i >= 1),
-                lambda: kv_ahead(unit, way, d, i).wait_send(),
-            )
-
-    for unit in range(2):
+        when(jnp.logical_and(has_ahead, groups[unit] >= 1), lambda: kv_ahead(unit, way, d).wait_send())
+
+    for unit in range(QUAD):
         for way in (0, 1):
             when(goes_on(way), lambda: kv_line(unit, way, 0).wait_send())
         sent_ahead(unit, 0, 0)
@@ -427,7 +422,7 @@
     bf16 = jnp.bfloat16
     return pl.pallas_call(
         functools.partial(gather_kernel, seq, fsdp, parts),
-        in_specs=[far, vmem, far, far, far],
+        in_specs=[far] * 5,
         out_specs=[anywhere, anywhere, vmem],
         out_shape=[
             jax.ShapeDtypeStruct((2, SPAN + QUAD, fsdp, rows, HD), bf16),
@@ -437,12 +432,13 @@
         scratch_shapes=[
             pltpu.VMEM((QUAD, rows, width), bf16),
             pltpu.VMEM((fsdp, 2, depth, 2 * HD), bf16),
-            pltpu.VMEM((2, 2, 2, rows, HD), bf16),
+            pltpu.VMEM((QUAD, 2, rows, HD), bf16),
             pltpu.VMEM((QUAD, 8, LINE), jnp.int32),
             pltpu.VMEM((rows, WIDE), bf16),
             pltpu.VMEM(docs.shape, jnp.int32),
             pltpu.VMEM(docs.shape, jnp.int32),
-            dma((8,)),
+            pltpu.VMEM(docs.shape, jnp.int32),
+            dma((9,)),
             dma((3, parts)),
             dma((3, parts)),
             dma((3,)),
@@ -453,17 +449,17 @@
             dma((2, fsdp + 1, 2)),
             dma((2, fsdp, 2)),
             dma((2, fsdp, 2)),
-            dma((2, 2, fsdp)),
-            dma((2, 2, fsdp + 1)),
-            dma((2, 2 * fsdp, 2)),
-            dma((2, 2 * fsdp, 2)),
-            dma((2,)),
+            dma((QUAD, 2, fsdp)),
+            dma((QUAD, 2, fsdp + 1)),
+            dma((QUAD, 2 * fsdp)),
+            dma((QUAD, 2 * fsdp)),
+            dma((QUAD,)),
         ],
         compiler_params=pltpu.CompilerParams(
             collective_id=0, has_side_effects=True, vmem_limit_bytes=32 * 1024 * 1024
         ),
         name="gather",
-    )(marked, docs, *(pltpu.with_memory_space_constraint(x, pltpu.HBM) for x in (hidden, kv_weights, queries)))
+    )(marked, *(pltpu.with_memory_space_constraint(x, pltpu.HBM) for x in (docs, hidden, kv_weights, queries)))
 
 
 def attend_kernel(key_block, slot, limits_ref, q_ref, k_ref, after_ref, out_ref, qt, top, total, acc):

time: 114 us -> 114 us (level)
  starting transfers between devices: 8.68 us -> 7.28 us
  Pallas kernels: 96.8 us -> 98 us
    ppermute x3, starting transfers between devices: 8.68 us -> 7.28 us  [local(): pieces[slot] = lax.ppermute(mixed, 'seq', swap) if slot else mixed]
    pallas_call x1, Pallas kernels: 80.5 us -> 81.8 us  [gather(): pl.pallas_call(functools.partial(gather_kernel, seq, fsdp, parts), in_spe...]
where the time goes in v1:
time: 114 us; the launch traced here: 113 us
  Pallas kernels  98 us (86%)
  starting transfers between devices  7.28 us (6%)
  waiting for transfers between devices  6.37 us (6%)
    pallas_call x1, Pallas kernels, gather(): pl.pallas_call(functools.partial(gather_kernel, seq, fsdp, parts), in_spe...  81.8 us
    pallas_call x4, Pallas kernels, attend(): pl.pallas_call(functools.partial(attend_kernel, key_block, slot), in_spec...  15.2 us
    ppermute x3, starting transfers between devices, local(): pieces[slot] = lax.ppermute(mixed, 'seq', swap) if slot else mixed  7.28 us
    ppermute x3, waiting for transfers between devices, local(): pieces[slot] = lax.ppermute(mixed, 'seq', swap) if slot else mixed  6.37 us
  transfers between devices with their start and end apart: 3, of which 2 were waited for; matrix products, arithmetic and copies ran while one was open for 0% of the time, Pallas kernels for 5%

profile of v1, /device:TPU:5, one launch (start us, length us, event | category | flops | bytes accessed | tf_op | source)
XLA Modules:
  0.0 112.5 jit_solution(8148345684812349855)
XLA Ops:
  0.7 81.8 %gather.1 = (bf16[2,7,4,256,128]{4,3,2,1,0:T(8,128)(2,1)S(1)}, bf16[4,256,512]{2,1,0:T(8,128)(2,1)S(1)}, s32[8,256]{1,0:T(8,128)S(1)}) custom-call(s32[8,128]{1,0:T(8,128)S(1)} %broadcast_in_dim.3.mod_ref, s32[64,128]{1,0:T(8,128)} %bitcast.8, bf16[256,3584]{1,0:T(8,128)(2,1)} %hidden_ref.1, bf16[2,896,1024]{2,1,0:T(8,128)(2,1)} %w_ref.1, ...), custom_call_target="tpu_custom_call" | custom-call | tf_op jit(solution)/shard_map/gather/pallas_call | solution.py:423
  82.5 2.5 %shard_map.55.after_ref = bf16[256,512]{1,0:T(8,128)(2,1)S(1)} custom-call(s32[8,256]{1,0:T(8,128)S(1)} %get-tuple-element.8.limits_ref.after_ref, bf16[4,256,512]{2,1,0:T(8,128)(2,1)S(1)} %get-tuple-element.9.q_ref, bf16[2,7168,128]{2,1,0:T(8,128)(2,1)S(1)} %bitcast.4, s32[8,256]{1,0:T(8,128)S(1)} %get-tuple-element.8.limits_ref.after_ref), custom_call_target="tpu_custom_call" | custom-call | flops 939524096 | bytes 3670016 | tf_op jit(solution)/shard_map/pallas_call | solution.py:533
  85.0 3.5 %shard_map.56.after_ref = bf16[256,512]{1,0:T(8,128)(2,1)S(1)} custom-call(s32[8,256]{1,0:T(8,128)S(1)} %get-tuple-element.8.limits_ref.after_ref, bf16[4,256,512]{2,1,0:T(8,128)(2,1)S(1)} %get-tuple-element.9.q_ref, bf16[2,7168,128]{2,1,0:T(8,128)(2,1)S(1)} %bitcast.5, bf16[256,512]{1,0:T(8,128)(2,1)S(1)} %shard_map.55.after_ref), custom_call_target="tpu_custom_call" | custom-call | flops 939524096 | bytes 3670016 | tf_op jit(solution)/shard_map/pallas_call | solution.py:533
  88.5 3.7 %shard_map.57.after_ref = bf16[256,512]{1,0:T(8,128)(2,1)S(1)} custom-call(s32[8,256]{1,0:T(8,128)S(1)} %get-tuple-element.8.limits_ref.after_ref, bf16[4,256,512]{2,1,0:T(8,128)(2,1)S(1)} %get-tuple-element.9.q_ref, bf16[2,7168,128]{2,1,0:T(8,128)(2,1)S(1)} %bitcast.6, bf16[256,512]{1,0:T(8,128)(2,1)S(1)} %shard_map.56.after_ref), custom_call_target="tpu_custom_call" | custom-call | flops 939524096 | bytes 3670016 | tf_op jit(solution)/shard_map/pallas_call | solution.py:533
  92.2 5.6 %collective-permute-start = (bf16[256,512]{1,0:T(8,128)(2,1)S(1)}, bf16[256,512]{1,0:T(8,128)(2,1)S(1)}, u32[]{:S(2)}, u32[]{:S(2)}) collective-permute-start(bf16[256,512]{1,0:T(8,128)(2,1)S(1)} %shard_map.57.after_ref), channel_id=1, source_target_pairs={{0,4},{4,0},{8,12},{12,8},{16,20},{20,16},{24,28},{28,24},{1,5},{5... | collective-permute-start | bytes 786440 | tf_op jit(solution)/shard_map/ppermute | solution.py:586
  97.7 0.0 collective-permute-start.1
  97.7 1.7 %collective-permute-start.2 = (bf16[256,512]{1,0:T(8,128)(2,1)S(1)}, bf16[256,512]{1,0:T(8,128)(2,1)S(1)}, u32[]{:S(2)}, u32[]{:S(2)}) collective-permute-start(bf16[256,512]{1,0:T(8,128)(2,1)S(1)} %shard_map.55.after_ref), channel_id=1, source_target_pairs={{0,12},{4,8},{8,4},{12,0},{16,28},{20,24},{24,20},{28,16},{1,13},{... | collective-permute-start | bytes 786440 | tf_op jit(solution)/shard_map/ppermute | solution.py:586
  99.5 5.6 %shard_map.58.refs_0_ = bf16[256,512]{1,0:T(8,128)(2,1)S(1)} custom-call(s32[8,256]{1,0:T(8,128)S(1)} %get-tuple-element.8.limits_ref.after_ref, bf16[4,256,512]{2,1,0:T(8,128)(2,1)S(1)} %get-tuple-element.9.q_ref, bf16[2,7168,128]{2,1,0:T(8,128)(2,1)S(1)} %bitcast.7, bf16[256,512]{1,0:T(8,128)(2,1)S(1)} %shard_map.57.after_ref), custom_call_target="tpu_custom_call" | custom-call | flops 939524096 | bytes 3670016 | tf_op jit(solution)/shard_map/pallas_call | solution.py:533
  105.0 0.0 collective-permute-done.refs_1_
  105.0 0.5 collective-permute-done.1.refs_2_
  105.5 5.9 %collective-permute-done.2.refs_3_ = bf16[256,512]{1,0:T(8,128)(2,1)S(1)} collective-permute-done((bf16[256,512]{1,0:T(8,128)(2,1)S(1)}, bf16[256,512]{1,0:T(8,128)(2,1)S(1)}, u32[]{:S(2)}, u32[]{:S(2)}) %collective-permute-start.2) | collective-permute-done | bytes 262176 | tf_op jit(solution)/shard_map/ppermute | solution.py:586
  111.4 1.0 assemble.1
  (1 shorter events, 0.0 us)
Async XLA Ops:
  92.2 12.8 %collective-permute-start = (bf16[256,512]{1,0:T(8,128)(2,1)S(1)}, bf16[256,512]{1,0:T(8,128)(2,1)S(1)}, u32[]{:S(2)}, u32[]{:S(2)}) collective-permute-start(bf16[256,512]{1,0:T(8,128)(2,1)S(1)} %shard_map.57.after_ref), channel_id=1, source_target_pairs={{0,4},{4,0},{8,12},{12,8},{16,20},{20,16},{24,28},{28,24},{1,5},{5... | collective-permute-start | bytes 786440 | tf_op jit(solution)/shard_map/ppermute | solution.py:586
  97.7 7.8 %collective-permute-start.1 = (bf16[256,512]{1,0:T(8,128)(2,1)S(1)}, bf16[256,512]{1,0:T(8,128)(2,1)S(1)}, u32[]{:S(2)}, u32[]{:S(2)}) collective-permute-start(bf16[256,512]{1,0:T(8,128)(2,1)S(1)} %shard_map.56.after_ref), channel_id=1, source_target_pairs={{0,8},{4,12},{8,0},{12,4},{16,24},{20,28},{24,16},{28,20},{1,9},{5... | collective-permute-start | bytes 786440 | tf_op jit(solution)/shard_map/ppermute | solution.py:586
  97.7 13.6 %collective-permute-start.2 = (bf16[256,512]{1,0:T(8,128)(2,1)S(1)}, bf16[256,512]{1,0:T(8,128)(2,1)S(1)}, u32[]{:S(2)}, u32[]{:S(2)}) collective-permute-start(bf16[256,512]{1,0:T(8,128)(2,1)S(1)} %shard_map.55.after_ref), channel_id=1, source_target_pairs={{0,12},{4,8},{8,4},{12,0},{16,28},{20,24},{24,20},{28,16},{1,13},{... | collective-permute-start | bytes 786440 | tf_op jit(solution)/shard_map/ppermute | solution.py:586

commit v2 on v1

--- a/solution.py
+++ b/solution.py
@@ -76,7 +76,7 @@
             keep.append(
                 pltpu.make_async_copy(
                     w_ref.at[m, :, columns(h, half)],
-                    w.at[z, m, :, half * HD : (half + 1) * HD],
+                    w.at[z, m, half],
                     local.at[1 + 2 * m + half],
                 )
             )
@@ -103,13 +103,12 @@
     pl.semaphore_wait(barrier, len(near) + both)
 
     def w_slot(zs, m, half):
-        return w.at[zs, m, :, half * HD : (half + 1) * HD]
+        return w.at[zs, m, half]
 
     def w_line(way, d, half):
-        src = w_ref.at[carried, :, columns(h, half)] if d == 0 else w_slot(source(way, d), carried, half)
         zs = z if d == 0 else source(way, d)
         return remote(
-            src, w_slot(zs, carried, half), wz_send.at[way, d, half], wz_recv.at[way, d + 1, half], onward(way)
+            w_slot(zs, carried, half), w_slot(zs, carried, half), wz_send.at[way, d, half], wz_recv.at[way, d + 1, half], onward(way)
         )
 
     def w_arrived(way, d, half):
@@ -163,7 +162,8 @@
         slot = q_out.at[1 + i]
         return remote(slot, slot, q_send.at[i], q_recv.at[i], (mates[i], z))
 
-    groups = [flip(s, unit) - base for unit in range(QUAD)]
+    side = lax.div(h, 2)
+    groups = [2 * side + 1, 2 * side, 3 - 2 * side, 2 - 2 * side]
 
     def kv_slot(unit, zs):
         return kv_out.at[:, SPAN + groups[unit], zs]
@@ -205,6 +205,8 @@
             act()
 
     for half in range(2):
+        keep[1 + half].wait()
+        keep[3 + half].wait()
         for way in (0, 1):
             when(goes_on(way), lambda: w_line(way, 0, half).start())
     for i in range(3):
@@ -246,7 +248,8 @@
         image = jnp.max(mods[group]) == 1
         total = None
         for zs in range(fsdp):
-            weight = jnp.where(image, w[zs, 1], w[zs, 0])
+            halves = [jnp.where(image, w[zs, 1, half], w[zs, 0, half]) for half in range(2)]
+            weight = jnp.concatenate(halves, axis=1)
             rows_at = hid[group, :, zs * depth : (zs + 1) * depth]
             term = jnp.dot(rows_at, weight, preferred_element_type=jnp.float32)
             total = term if total is None else total + term
@@ -287,8 +290,7 @@
         if done < parts - 2:
             pass_hidden(done)
             done += 1
-    for copy in keep:
-        copy.wait()
+    keep[0].wait()
     for part in range(parts):
         hid_got(0, twin, part).wait_recv()
     for way, d in lines:
@@ -313,16 +315,21 @@
     for part in range(parts):
         hid_got(2, diag, part).wait_recv()
     project(2)
-    relay(1, 2)
     project(3)
     send_made(2)
     send_made(3)
     for d in range(3, fsdp):
         relay(0, d)
+
+    def relay_late():
+        for d in range(1, fsdp):
+            relay(2, d)
+            relay(3, d)
+
+    when(side == 0, relay_late)
+    for d in range(2, fsdp):
         relay(1, d)
-    for d in range(1, fsdp):
-        relay(2, d)
-        relay(3, d)
+    when(side == 1, relay_late)
     for i in range(3):
         q_got(i).wait_recv()
     for unit in range(QUAD):
@@ -431,7 +438,7 @@
         ],
         scratch_shapes=[
             pltpu.VMEM((QUAD, rows, width), bf16),
-            pltpu.VMEM((fsdp, 2, depth, 2 * HD), bf16),
+            pltpu.VMEM((fsdp, 2, 2, depth, HD), bf16),
             pltpu.VMEM((QUAD, 2, rows, HD), bf16),
             pltpu.VMEM((QUAD, 8, LINE), jnp.int32),
             pltpu.VMEM((rows, WIDE), bf16),

time: 114 us -> 112 us (0.982)
  no operation moved by 1% of the time
where the time goes in v2:
time: 112 us; the launch traced here: 111 us
  Pallas kernels  97.2 us (87%)
  starting transfers between devices  6.49 us (6%)
  waiting for transfers between devices  6.37 us (6%)
    pallas_call x1, Pallas kernels, gather(): pl.pallas_call(functools.partial(gather_kernel, seq, fsdp, parts), in_spe...  81 us
    pallas_call x4, Pallas kernels, attend(): pl.pallas_call(functools.partial(attend_kernel, key_block, slot), in_spec...  15.3 us
    ppermute x3, starting transfers between devices, local(): pieces[slot] = lax.ppermute(mixed, 'seq', swap) if slot else mixed  6.49 us
    ppermute x3, waiting for transfers between devices, local(): pieces[slot] = lax.ppermute(mixed, 'seq', swap) if slot else mixed  6.37 us
  transfers between devices with their start and end apart: 3, of which 2 were waited for; matrix products, arithmetic and copies ran while one was open for 0% of the time, Pallas kernels for 5%

profile of v2, /device:TPU:5, one launch (start us, length us, event | category | flops | bytes accessed | tf_op | source)
XLA Modules:
  0.0 111.0 jit_solution(9079574144459450943)
XLA Ops:
  0.7 81.0 %gather.1 = (bf16[2,7,4,256,128]{4,3,2,1,0:T(8,128)(2,1)S(1)}, bf16[4,256,512]{2,1,0:T(8,128)(2,1)S(1)}, s32[8,256]{1,0:T(8,128)S(1)}) custom-call(s32[8,128]{1,0:T(8,128)S(1)} %broadcast_in_dim.3.mod_ref, s32[64,128]{1,0:T(8,128)} %bitcast.8, bf16[256,3584]{1,0:T(8,128)(2,1)} %hidden_ref.1, bf16[2,896,1024]{2,1,0:T(8,128)(2,1)} %w_ref.1, ...), custom_call_target="tpu_custom_call" | custom-call | tf_op jit(solution)/shard_map/gather/pallas_call | solution.py:430
  81.6 2.5 %shard_map.55.after_ref = bf16[256,512]{1,0:T(8,128)(2,1)S(1)} custom-call(s32[8,256]{1,0:T(8,128)S(1)} %get-tuple-element.8.limits_ref.after_ref, bf16[4,256,512]{2,1,0:T(8,128)(2,1)S(1)} %get-tuple-element.9.q_ref, bf16[2,7168,128]{2,1,0:T(8,128)(2,1)S(1)} %bitcast.4, s32[8,256]{1,0:T(8,128)S(1)} %get-tuple-element.8.limits_ref.after_ref), custom_call_target="tpu_custom_call" | custom-call | flops 939524096 | bytes 3670016 | tf_op jit(solution)/shard_map/pallas_call | solution.py:540
  84.1 3.5 %shard_map.56.after_ref = bf16[256,512]{1,0:T(8,128)(2,1)S(1)} custom-call(s32[8,256]{1,0:T(8,128)S(1)} %get-tuple-element.8.limits_ref.after_ref, bf16[4,256,512]{2,1,0:T(8,128)(2,1)S(1)} %get-tuple-element.9.q_ref, bf16[2,7168,128]{2,1,0:T(8,128)(2,1)S(1)} %bitcast.5, bf16[256,512]{1,0:T(8,128)(2,1)S(1)} %shard_map.55.after_ref), custom_call_target="tpu_custom_call" | custom-call | flops 939524096 | bytes 3670016 | tf_op jit(solution)/shard_map/pallas_call | solution.py:540
  87.7 3.7 %shard_map.57.after_ref = bf16[256,512]{1,0:T(8,128)(2,1)S(1)} custom-call(s32[8,256]{1,0:T(8,128)S(1)} %get-tuple-element.8.limits_ref.after_ref, bf16[4,256,512]{2,1,0:T(8,128)(2,1)S(1)} %get-tuple-element.9.q_ref, bf16[2,7168,128]{2,1,0:T(8,128)(2,1)S(1)} %bitcast.6, bf16[256,512]{1,0:T(8,128)(2,1)S(1)} %shard_map.56.after_ref), custom_call_target="tpu_custom_call" | custom-call | flops 939524096 | bytes 3670016 | tf_op jit(solution)/shard_map/pallas_call | solution.py:540
  91.4 4.8 %collective-permute-start = (bf16[256,512]{1,0:T(8,128)(2,1)S(1)}, bf16[256,512]{1,0:T(8,128)(2,1)S(1)}, u32[]{:S(2)}, u32[]{:S(2)}) collective-permute-start(bf16[256,512]{1,0:T(8,128)(2,1)S(1)} %shard_map.57.after_ref), channel_id=1, source_target_pairs={{0,4},{4,0},{8,12},{12,8},{16,20},{20,16},{24,28},{28,24},{1,5},{5... | collective-permute-start | bytes 786440 | tf_op jit(solution)/shard_map/ppermute | solution.py:593
  96.2 0.0 collective-permute-start.1
  96.2 1.7 %collective-permute-start.2 = (bf16[256,512]{1,0:T(8,128)(2,1)S(1)}, bf16[256,512]{1,0:T(8,128)(2,1)S(1)}, u32[]{:S(2)}, u32[]{:S(2)}) collective-permute-start(bf16[256,512]{1,0:T(8,128)(2,1)S(1)} %shard_map.55.after_ref), channel_id=1, source_target_pairs={{0,12},{4,8},{8,4},{12,0},{16,28},{20,24},{24,20},{28,16},{1,13},{... | collective-permute-start | bytes 786440 | tf_op jit(solution)/shard_map/ppermute | solution.py:593
  97.9 5.6 %shard_map.58.refs_0_ = bf16[256,512]{1,0:T(8,128)(2,1)S(1)} custom-call(s32[8,256]{1,0:T(8,128)S(1)} %get-tuple-element.8.limits_ref.after_ref, bf16[4,256,512]{2,1,0:T(8,128)(2,1)S(1)} %get-tuple-element.9.q_ref, bf16[2,7168,128]{2,1,0:T(8,128)(2,1)S(1)} %bitcast.7, bf16[256,512]{1,0:T(8,128)(2,1)S(1)} %shard_map.57.after_ref), custom_call_target="tpu_custom_call" | custom-call | flops 939524096 | bytes 3670016 | tf_op jit(solution)/shard_map/pallas_call | solution.py:540
  103.4 0.0 collective-permute-done.refs_1_
  103.4 0.5 collective-permute-done.1.refs_2_
  103.9 5.9 %collective-permute-done.2.refs_3_ = bf16[256,512]{1,0:T(8,128)(2,1)S(1)} collective-permute-done((bf16[256,512]{1,0:T(8,128)(2,1)S(1)}, bf16[256,512]{1,0:T(8,128)(2,1)S(1)}, u32[]{:S(2)}, u32[]{:S(2)}) %collective-permute-start.2) | collective-permute-done | bytes 262176 | tf_op jit(solution)/shard_map/ppermute | solution.py:593
  109.8 1.0 assemble.1
  (1 shorter events, 0.0 us)
Async XLA Ops:
  91.4 12.1 %collective-permute-start = (bf16[256,512]{1,0:T(8,128)(2,1)S(1)}, bf16[256,512]{1,0:T(8,128)(2,1)S(1)}, u32[]{:S(2)}, u32[]{:S(2)}) collective-permute-start(bf16[256,512]{1,0:T(8,128)(2,1)S(1)} %shard_map.57.after_ref), channel_id=1, source_target_pairs={{0,4},{4,0},{8,12},{12,8},{16,20},{20,16},{24,28},{28,24},{1,5},{5... | collective-permute-start | bytes 786440 | tf_op jit(solution)/shard_map/ppermute | solution.py:593
  96.2 7.8 %collective-permute-start.1 = (bf16[256,512]{1,0:T(8,128)(2,1)S(1)}, bf16[256,512]{1,0:T(8,128)(2,1)S(1)}, u32[]{:S(2)}, u32[]{:S(2)}) collective-permute-start(bf16[256,512]{1,0:T(8,128)(2,1)S(1)} %shard_map.56.after_ref), channel_id=1, source_target_pairs={{0,8},{4,12},{8,0},{12,4},{16,24},{20,28},{24,16},{28,20},{1,9},{5... | collective-permute-start | bytes 786440 | tf_op jit(solution)/shard_map/ppermute | solution.py:593
  96.2 13.6 %collective-permute-start.2 = (bf16[256,512]{1,0:T(8,128)(2,1)S(1)}, bf16[256,512]{1,0:T(8,128)(2,1)S(1)}, u32[]{:S(2)}, u32[]{:S(2)}) collective-permute-start(bf16[256,512]{1,0:T(8,128)(2,1)S(1)} %shard_map.55.after_ref), channel_id=1, source_target_pairs={{0,12},{4,8},{8,4},{12,0},{16,28},{20,24},{24,20},{28,16},{1,13},{... | collective-permute-start | bytes 786440 | tf_op jit(solution)/shard_map/ppermute | solution.py:593
